TPU v7x, 32 devices: a whole 2x2x4 slice. The times are simulated.
32 devices in a mesh: parts: 2 (over y), row: 4 (over x, core), col: 4 (over z).
Axes of the slice: x: 2, y: 2, z: 4, core: 2. Of those that a mesh axis runs over, the one named last changes fastest.
Arguments:
- latent: bfloat16 [4, 32, 32, 640], P('parts', 'row', 'col'), parts along dimension 0, may hold values from -6 to 6
- timestep: int32 [4], P('parts'), parts along dimension 0, may hold values from 0 to 999
- gn_gain: float32 [640], replicated, may hold values from 0.25 to 1.75
- gn_bias: float32 [640], replicated, may hold values from -3 to 3
- conv_weight: bfloat16 [3, 3, 640, 640], P(None, None, None, 'row'), may hold values from -0.078125 to 0.078125
- conv_bias: float32 [640], replicated, may hold values from -3 to 3
- time_weight: bfloat16 [320, 640], replicated, may hold values from -0.625 to 0.625
- ln_gain: float32 [640], replicated, may hold values from 0.25 to 1.75
- q_weight: bfloat16 [640, 384], replicated, may hold values from -0.5 to 0.5
- k_weight: bfloat16 [640, 384], replicated, may hold values from -0.25 to 0.25
- v_weight: bfloat16 [640, 384], replicated, may hold values from -0.25 to 0.25
- out_weight: bfloat16 [384, 640], replicated, may hold values from -0.3125 to 0.3125
- stale_keys: bfloat16 [4, 32, 32, 384], P('parts', 'row', 'col'), parts along dimension 0, may hold values from -40 to 40
- stale_values: bfloat16 [4, 32, 32, 384], P('parts', 'row', 'col'), parts along dimension 0, may hold values from -6 to 6
Outputs:
- mixed: bfloat16 [4, 32, 32, 640], P('parts', 'row', 'col'), parts along dimension 0
- fresh_keys: bfloat16 [4, 32, 32, 384], P('parts', 'row', 'col'), parts along dimension 0
- fresh_values: bfloat16 [4, 32, 32, 384], P('parts', 'row', 'col'), parts along dimension 0
There are 2 independent parts, one for each index of `parts`. A program takes and returns all parts, laid end to end along the dimension named above; an argument that names none is the same for every part. Nothing has to cross between parts.
All inputs are finite; a program needn't handle non-finite values.
Results may differ from a plain program's by a relative error of at most 0.012.
Values may be sent and summed in bfloat16 or wider, within the bound.
A program may use at most 64 MiB of HBM per device.

v0:
```python
import jax
import jax.numpy as jnp
from jax import lax
from jax.sharding import PartitionSpec as P

HD = 64
GROUPS = 32


def with_halo(cells, sides, width):
    for axis, dim in sides:
        count = lax.axis_size(axis)
        ends = count - 1
        head = lax.slice_in_dim(cells, 0, width, axis=dim)
        tail = lax.slice_in_dim(cells, cells.shape[dim] - width, cells.shape[dim], axis=dim)
        cells = jnp.concatenate(
            [
                lax.ppermute(tail, axis, [(i, (i + 1) % count) for i in range(ends)]),
                cells,
                lax.ppermute(head, axis, [((i + 1) % count, i) for i in range(ends)]),
            ],
            axis=dim,
        )
    return cells


def time_features(timestep, width):
    half = width // 2
    freqs = jnp.exp(-jnp.log(10000.0) * jnp.arange(half, dtype=jnp.float32) / half)
    angles = timestep.astype(jnp.float32)[:, None] * freqs[None, :]
    return jnp.concatenate([jnp.cos(angles), jnp.sin(angles)], axis=1)


def make_fold(query_all, own_query, own_key, span, heads):
    batch, rows_q, inner = query_all.shape
    head_size = inner // heads
    query_heads = query_all.reshape(batch, rows_q, heads, head_size)
    query_block = jnp.arange(rows_q, dtype=jnp.int32) // span

    def fold(carry, pieces, start):
        keys_piece, values_piece = pieces
        count = keys_piece.shape[1]
        width = 128
        keys_blocks = keys_piece.reshape(batch, count // width, width, heads, head_size).transpose(
            1, 0, 2, 3, 4
        )
        values_blocks = values_piece.reshape(
            batch, count // width, width, heads, head_size
        ).transpose(1, 0, 2, 3, 4)
        offsets = width * jnp.arange(count // width, dtype=jnp.int32)

        def step(state, items):
            peak, total, summed = state
            keys_block, values_block, offset = items
            scores = jnp.einsum(
                "bqhd,bkhd->bhqk", query_heads, keys_block, preferred_element_type=jnp.float32
            )
            key_block = (offset + jnp.arange(width, dtype=jnp.int32)) // span
            masked = (query_block == own_query)[:, None] & (key_block == own_key)[None, :]
            scores = jnp.where(masked, -1e30, scores)
            new_peak = jnp.maximum(peak, jnp.max(scores, axis=-1))
            weights = jnp.where(masked, 0.0, jnp.exp(scores - new_peak[..., None]))
            factor = jnp.exp(peak - new_peak)
            total = total * factor + jnp.sum(weights, axis=-1)
            summed = summed * factor[..., None] + jnp.einsum(
                "bhqk,bkhd->bhqd",
                weights.astype(jnp.bfloat16),
                values_block,
                preferred_element_type=jnp.float32,
            )
            return ((new_peak, total, summed), None)

        result, unused = lax.scan(step, carry, (keys_blocks, values_blocks, offsets))
        return result

    return fold


def body(
    latent,
    timestep,
    gn_gain,
    gn_bias,
    conv_weight,
    conv_bias,
    time_weight,
    ln_gain,
    q_weight,
    k_weight,
    v_weight,
    out_weight,
    stale_keys,
    stale_values,
):
    batch, rows, columns, channels = latent.shape
    inner = q_weight.shape[1]
    heads = inner // HD
    span = rows * columns
    count_all = span * lax.axis_size("row") * lax.axis_size("col") * (channels // GROUPS)
    emb = jax.nn.silu(time_features(timestep, time_weight.shape[0])).astype(jnp.bfloat16)
    temb = jnp.dot(emb, time_weight, preferred_element_type=jnp.float32)
    values = latent.astype(jnp.float32)
    grouped = values.reshape(batch, span, GROUPS, channels // GROUPS)
    sum_one = jnp.sum(grouped, axis=(1, 3))
    sum_two = jnp.sum(grouped * grouped, axis=(1, 3))
    total_one, total_two = lax.psum((sum_one, sum_two), ("row", "col"))
    mean = total_one / count_all
    var = total_two / count_all - mean * mean
    normed = (grouped - mean[:, None, :, None]) * lax.rsqrt(var + 1e-05)[:, None, :, None]
    normed = normed.reshape(batch, rows, columns, channels) * gn_gain + gn_bias
    act = jax.nn.silu(normed).astype(jnp.bfloat16)
    padded = with_halo(act, (("row", 1), ("col", 2)), 1)
    piece = lax.all_gather(conv_weight, "row", axis=3, tiled=True)
    result = jnp.zeros((batch, rows, columns, piece.shape[3]), jnp.float32)
    for down in range(3):
        for across in range(3):
            result = result + jnp.dot(
                padded[:, down : down + rows, across : across + columns, :],
                piece[down, across],
                preferred_element_type=jnp.float32,
            )
    hidden = (values + result + conv_bias + temb[:, None, None, :]).astype(jnp.bfloat16)
    hidden_f = hidden.astype(jnp.float32)
    centre = hidden_f - jnp.mean(hidden_f, axis=-1, keepdims=True)
    spread = jnp.mean(centre * centre, axis=-1, keepdims=True)
    layer_normed = (centre * lax.rsqrt(spread + 1e-05) * ln_gain).astype(jnp.bfloat16)
    queries = (
        jnp.dot(layer_normed, q_weight, preferred_element_type=jnp.float32)
        * (1.0 / jnp.sqrt(jnp.float32(HD)))
    ).astype(jnp.bfloat16)
    fresh_keys = jnp.dot(layer_normed, k_weight, preferred_element_type=jnp.float32).astype(
        jnp.bfloat16
    )
    fresh_values = jnp.dot(layer_normed, v_weight, preferred_element_type=jnp.float32).astype(
        jnp.bfloat16
    )
    query_rows = queries.reshape(batch, span, inner)
    stale_k = stale_keys.reshape(batch, span, inner)
    stale_v = stale_values.reshape(batch, span, inner)
    own_q = query_rows.reshape(batch, span, heads, HD)
    own_k = fresh_keys.reshape(batch, span, heads, HD)
    own_v = fresh_values.reshape(batch, span, heads, HD)
    own_scores = jnp.einsum("bqhd,bkhd->bhqk", own_q, own_k, preferred_element_type=jnp.float32)
    own_peak = jnp.max(own_scores, axis=-1)
    query_all = lax.all_gather(query_rows, "col", axis=1, tiled=True)
    query_index = lax.axis_index("col")
    key_index = lax.axis_index("row")
    rows_q = query_all.shape[1]
    initial = (
        jnp.full((batch, heads, rows_q), -1e30, jnp.float32),
        jnp.zeros((batch, heads, rows_q), jnp.float32),
        jnp.zeros((batch, heads, rows_q, HD), jnp.float32),
    )
    fold = make_fold(query_all, query_index, key_index, span, heads)
    peak, total, summed = fold(
        initial,
        (
            lax.all_gather(stale_k, "row", axis=1, tiled=True),
            lax.all_gather(stale_v, "row", axis=1, tiled=True),
        ),
        jnp.int32(0),
    )
    mine = lax.dynamic_slice_in_dim(peak, query_index * span, span, 2)
    raised = lax.dynamic_update_slice_in_dim(
        peak, jnp.maximum(mine, own_peak), query_index * span, 2
    )
    top = lax.pmax(raised.astype(jnp.bfloat16), "col").astype(raised.dtype)
    factor = jnp.exp(peak - top)
    scaled_sum = summed * factor[..., None]
    scaled_total = total * factor
    part_sum, part_total = (
        lax.psum_scatter(
            scaled_sum.astype(jnp.bfloat16), "col", scatter_dimension=2, tiled=True
        ).astype(jnp.float32),
        lax.psum_scatter(
            scaled_total.astype(jnp.bfloat16), "col", scatter_dimension=2, tiled=True
        ).astype(jnp.float32),
    )
    top_own = lax.dynamic_slice_in_dim(top, query_index * span, span, 2)
    own_weights = jnp.exp(own_scores - top_own[..., None])
    part_total = part_total + jnp.sum(own_weights, axis=-1)
    part_sum = part_sum + jnp.einsum(
        "bhqk,bkhd->bhqd",
        own_weights.astype(jnp.bfloat16),
        own_v,
        preferred_element_type=jnp.float32,
    )
    attn = (
        (part_sum / part_total[..., None])
        .transpose(0, 2, 1, 3)
        .reshape(batch, span, inner)
        .astype(jnp.bfloat16)
    )
    mixed = hidden_f.reshape(batch, span, channels) + jnp.dot(
        attn, out_weight, preferred_element_type=jnp.float32
    )
    mixed = mixed.astype(jnp.bfloat16).reshape(batch, rows, columns, channels)
    return (mixed, fresh_keys, fresh_values)


def solution(mesh):
    placed = (
        P("parts", "row", "col", None),
        P("parts"),
        P(),
        P(),
        P(None, None, None, "row"),
        P(),
        P(),
        P(),
        P(),
        P(),
        P(),
        P(),
        P("parts", "row", "col", None),
        P("parts", "row", "col", None),
    )
    return jax.shard_map(
        body,
        mesh=mesh,
        in_specs=placed,
        out_specs=(
            P("parts", "row", "col", None),
            P("parts", "row", "col", None),
            P("parts", "row", "col", None),
        ),
        check_vma=False,
    )
```

profile of v0, /device:TPU:0, one launch (start us, length us, event | category | flops | bytes accessed | tf_op | source)
XLA Modules:
  0.0 180.5 jit_solution(7372070736849188195)
XLA Ops:
  7.3 0.7 all-gather.2.cloned.1.call-update
  8.6 35.7 %all-reduce = (f32[2,32]{1,0:T(2,128)S(1)}, f32[2,32]{1,0:T(2,128)S(1)}) all-reduce(f32[2,32]{1,0:T(2,128)S(1)} %reduce_sum.76, f32[2,32]{1,0:T(2,128)S(1)} %reduce_sum.73), channel_id=1, replica_groups=mesh['parts'=2,'row'=4,'col'=4] {'row','col'}, use_global_device_ids=true, to_apply=%region_5.6 | all-reduce | flops 128 | bytes 1024 | tf_op jit(solution)/shard_map/psum | solution.py:106
  44.9 1.3 collective-permute-start
  46.2 1.3 collective-permute-start.1
  47.8 10.8 %all_gather.13 = bf16[2,256,384]{2,0,1:T(2,128)(2,1)S(1)} all-gather(bf16[2,64,384]{2,0,1:T(2,128)(2,1)S(1)} %bitcast.148), channel_id=1, replica_groups=mesh['parts'=2,'row'=4,'col'=4] {'row'}, dimensions={1}, use_global_device_ids=true | all-gather | bytes 491520 | tf_op jit(solution)/shard_map/all_gather | solution.py:158
  58.9 9.1 %all_gather.15 = bf16[2,256,384]{2,0,1:T(2,128)(2,1)S(1)} all-gather(bf16[2,64,384]{2,0,1:T(2,128)(2,1)S(1)} %bitcast.147), channel_id=1, replica_groups=mesh['parts'=2,'row'=4,'col'=4] {'row'}, dimensions={1}, use_global_device_ids=true | all-gather | bytes 491520 | tf_op jit(solution)/shard_map/all_gather | solution.py:159
  68.0 1.3 collective-permute-start.2
  69.3 1.3 collective-permute-start.3
  70.7 0.5 copy.49
  71.3 0.8 copy.53
  72.1 0.5 copy.52
  72.7 0.8 copy.54
  73.5 1.8 %collective-permute-done.3 = bf16[2,10,1,640]{3,2,1,0:T(2,128)(2,1)S(1)} collective-permute-done((bf16[2,10,1,640]{3,2,1,0:T(2,128)(2,1)S(1)}, bf16[2,10,1,640]{3,2,1,0:T(2,128)(2,1)S(1)}, u32[]{:S(2)}, u32[]{:S(2)}) %collective-permute-start.3) | collective-permute-done | bytes 25632 | tf_op jit(solution)/shard_map/ppermute | solution.py:20
  75.6 1.5 fusion.41
  77.1 1.5 fusion.38
  78.6 1.5 fusion.39
  80.1 1.5 fusion.37
  81.6 1.5 fusion.40
  83.1 1.5 fusion.35
  84.7 1.5 fusion.36
  86.2 1.5 fusion.21
  87.7 1.7 fusion.86
  90.0 0.6 copy-done.8
  90.7 0.9 reshape.105
  91.5 1.3 fusion.34
  92.8 0.9 reshape_reshape.3
  93.7 15.4 %all_gather.14 = bf16[2,256,384]{2,1,0:T(8,128)(2,1)S(1)} all-gather(bf16[2,64,384]{2,1,0:T(8,128)(2,1)S(1)} %bitcast.145), channel_id=1, replica_groups=mesh['parts'=2,'row'=4,'col'=4] {'col'}, dimensions={1}, use_global_device_ids=true | all-gather | bytes 491520 | tf_op jit(solution)/shard_map/all_gather | solution.py:145
  109.3 8.7 %while.17 = (s32[]{:T(128)}, f32[2,6,256]{2,1,0:T(8,128)S(1)}, f32[2,6,256]{2,1,0:T(8,128)S(1)}, f32[2,6,256,64]{2,3,1,0:T(8,128)S(1)}, s32[]{:T(128)}, /*index=...) while((s32[]{:T(128)}, f32[2,6,256]{2,1,0:T(8,128)S(1)}, ...), condition=%wide.region_11.12_spmd.clone, body=%wide.region_8.11_spmd.clone.sunk | while | flops 104451456 | bytes 8988089 | solution.py:73
  109.3 0.7 dynamic_slice.48
  109.9 0.6 fusion.107
  110.7 1.4 fusion.108
  112.4 0.7 copy-done.3
  113.1 0.5 convolution_add_fusion.6
  113.6 0.7 dynamic_slice.48
  114.3 0.6 fusion.107
  115.0 1.4 fusion.108
  116.7 0.7 copy-done.3
  117.4 0.5 convolution_add_fusion.6
  117.9 1.3 fusion.87
  119.5 8.7 %pmax.7 = bf16[2,6,256]{2,1,0:T(8,128)(2,1)S(1)} all-reduce(bf16[2,6,256]{2,1,0:T(8,128)(2,1)S(1)} %convert_element_type.78), channel_id=1, replica_groups=mesh['parts'=2,'row'=4,'col'=4] {'col'}, use_global_device_ids=true, to_apply=%region_13.14 | all-reduce | flops 3072 | bytes 12288 | tf_op jit(solution)/shard_map/pmax | solution.py:167
  128.5 0.7 reshape.121
  129.3 0.5 copy.57
  129.8 1.4 multiply_convert_fusion
  131.8 15.8 %reduce-scatter.7.cloned.1.call-done = bf16[64,12]{1,0:T(8,128)(2,1)} async-done(((bf16[256,12]{1,0:T(8,128)(2,1)}), bf16[64,12]{1,0:T(8,128)(2,1)}) %reduce-scatter.7.cloned.1.call-update) | async-done | bytes 1552
  147.6 0.8 reshape.122
  148.5 23.0 %reduce-scatter.5.cloned.1.call-done = bf16[2,6,64,64]{3,2,1,0:T(8,128)(2,1)} async-done(((bf16[2,6,256,64]{3,2,1,0:T(8,128)(2,1)}), bf16[2,6,64,64]{3,2,1,0:T(8,128)(2,1)}) %reduce-scatter.5.cloned.1.call-update) | async-done | bytes 98320 | tf_op jit(solution)/shard_map/reduce_scatter | solution.py:172
  171.4 1.2 fusion.32
  173.0 0.9 fusion.33
  (101 shorter events, 5.4 us)
Async XLA Ops:
  7.2 165.9 %copy-start = (bf16[384,640]{1,0:T(8,128)(2,1)S(1)}, bf16[384,640]{1,0:T(8,128)(2,1)}, u32[]{:S(2)}) copy-start(bf16[384,640]{1,0:T(8,128)(2,1)} %param.27) | copy-start | bytes 1474564
  7.2 1.0 copy-start.4
  7.2 37.6 %copy-start.13 = (f32[640]{0:T(1024)S(1)}, f32[640]{0:T(1024)}, u32[]{:S(2)}) copy-start(f32[640]{0:T(1024)} %param.18) | copy-start | bytes 7684
  7.2 37.6 %copy-start.12 = (f32[640]{0:T(1024)S(1)}, f32[640]{0:T(1024)}, u32[]{:S(2)}) copy-start(f32[640]{0:T(1024)} %param.19) | copy-start | bytes 7684
  7.2 40.3 %copy-start.16 = (s32[2]{0:T(128)S(1)}, s32[2]{0:T(128)}, u32[]{:S(2)}) copy-start(s32[2]{0:T(128)} %param.17) | copy-start | bytes 28
  7.2 40.3 %copy-start.10 = (bf16[2,8,8,384]{3,2,1,0:T(8,128)(2,1)S(1)}, bf16[2,8,8,384]{3,2,1,0:T(8,128)(2,1)}, u32[]{:S(2)}) copy-start(bf16[2,8,8,384]{3,2,1,0:T(8,128)(2,1)} %param.28) | copy-start | bytes 294916
  7.2 40.4 %copy-start.11 = (bf16[2,8,8,384]{3,2,1,0:T(8,128)(2,1)S(1)}, bf16[2,8,8,384]{3,2,1,0:T(8,128)(2,1)}, u32[]{:S(2)}) copy-start(bf16[2,8,8,384]{3,2,1,0:T(8,128)(2,1)} %param.29) | copy-start | bytes 294916
  7.2 51.4 %copy-start.7 = (bf16[320,640]{1,0:T(8,128)(2,1)S(1)}, bf16[320,640]{1,0:T(8,128)(2,1)}, u32[]{:S(2)}) copy-start(bf16[320,640]{1,0:T(8,128)(2,1)} %param.22) | copy-start | bytes 1228804
  7.3 68.3 %all-gather.2.cloned.1.call-start = ((), (), s32[]{:S(2)}) async-start(), calls=%async_computation.2 | async-start | bytes 9216000 | tf_op jit(solution)/shard_map/all_gather | solution.py:113
  8.0 139.6 %reduce-scatter.7.cloned.1.call-start = ((), (), s32[]{:S(2)}) async-start(), calls=%async_computation.4 | async-start | bytes 81920
  44.9 23.0 %collective-permute-start = (bf16[2,1,8,640]{3,2,1,0:T(8,128)(2,1)S(1)}, bf16[2,1,8,640]{3,2,1,0:T(8,128)(2,1)S(1)}, u32[]{:S(2)}, u32[]{:S(2)}) collective-permute-start(bf16[2,1,8,640]{3,2,1,0:T(8,128)(2,1)S(1)} %get-tuple-element.235), channel_id=1, source_target_pairs={{0,4},{4,8},{8,12},{1,5},{5,9},{9,13},{2,6},{6,10},{10,14},{3,7},{... | collective-permute-start | bytes 61448 | tf_op jit(solution)/shard_map/ppermute | solution.py:18
  46.2 21.7 %collective-permute-start.1 = (bf16[2,1,8,640]{3,2,1,0:T(8,128)(2,1)S(1)}, bf16[2,1,8,640]{3,2,1,0:T(8,128)(2,1)S(1)}, u32[]{:S(2)}, u32[]{:S(2)}) collective-permute-start(bf16[2,1,8,640]{3,2,1,0:T(8,128)(2,1)S(1)} %get-tuple-element.236), channel_id=1, source_target_pairs={{4,0},{8,4},{12,8},{5,1},{9,5},{13,9},{6,2},{10,6},{14,10},{7,3},{... | collective-permute-start | bytes 61448 | tf_op jit(solution)/shard_map/ppermute | solution.py:20
  68.0 5.5 %collective-permute-start.2 = (bf16[2,10,1,640]{3,2,1,0:T(2,128)(2,1)S(1)}, bf16[2,10,1,640]{3,2,1,0:T(2,128)(2,1)S(1)}, u32[]{:S(2)}, u32[]{:S(2)}) collective-permute-start(bf16[2,10,1,640]{3,2,1,0:T(2,128)(2,1)S(1)} %get-tuple-element.233), channel_id=1, source_target_pairs={{0,1},{1,2},{2,3},{4,5},{5,6},{6,7},{8,9},{9,10},{10,11},{12,13},{... | collective-permute-start | bytes 76808 | tf_op jit(solution)/shard_map/ppermute | solution.py:18
  69.3 6.0 %collective-permute-start.3 = (bf16[2,10,1,640]{3,2,1,0:T(2,128)(2,1)S(1)}, bf16[2,10,1,640]{3,2,1,0:T(2,128)(2,1)S(1)}, u32[]{:S(2)}, u32[]{:S(2)}) collective-permute-start(bf16[2,10,1,640]{3,2,1,0:T(2,128)(2,1)S(1)} %get-tuple-element.234), channel_id=1, source_target_pairs={{1,0},{2,1},{3,2},{5,4},{6,5},{7,6},{9,8},{10,9},{11,10},{13,12},{... | collective-permute-start | bytes 76808 | tf_op jit(solution)/shard_map/ppermute | solution.py:20
  86.2 1.5 copy-start.14
  87.7 1.9 %copy-start.15 = (f32[640]{0:T(1024)S(1)}, f32[640]{0:T(1024)}, u32[]{:S(2)}) copy-start(f32[640]{0:T(1024)} %param.23) | copy-start | bytes 7684
  87.7 2.0 %copy-start.5 = (bf16[640,384]{1,0:T(8,128)(2,1)S(1)}, bf16[640,384]{1,0:T(8,128)(2,1)}, u32[]{:S(2)}) copy-start(bf16[640,384]{1,0:T(8,128)(2,1)} %param.25) | copy-start | bytes 1474564
  89.4 19.7 %copy-start.1 = (f32[2,8,8,640]{3,2,1,0:T(8,128)}, f32[2,8,8,640]{3,2,1,0:T(8,128)S(1)}, u32[]{:S(2)}) copy-start(f32[2,8,8,640]{3,2,1,0:T(8,128)S(1)} %get-tuple-element.242) | copy-start | bytes 983044
  90.0 0.6 copy-start.8
  112.1 1.0 copy-start.3
  116.4 1.0 copy-start.3
  129.2 42.2 %reduce-scatter.5.cloned.1.call-start = ((), (), s32[]{:S(2)}) async-start(), calls=%async_computation.3 | async-start | bytes 983040 | tf_op jit(solution)/shard_map/reduce_scatter | solution.py:172
  129.7 1.4 copy-start.6
  131.4 41.4 %copy-start.9 = (bf16[2,8,8,384]{3,2,1,0:T(8,128)(2,1)}, bf16[2,8,8,384]{3,2,1,0:T(8,128)(2,1)S(1)}, u32[]{:S(2)}) copy-start(bf16[2,8,8,384]{3,2,1,0:T(8,128)(2,1)S(1)} %convolution_convert_fusion) | copy-start | bytes 294916
  131.8 41.3 %copy-start.2 = (f32[2,8,8,640]{3,2,1,0:T(8,128)S(1)}, f32[2,8,8,640]{3,2,1,0:T(8,128)}, u32[]{:S(2)}) copy-start(f32[2,8,8,640]{3,2,1,0:T(8,128)} %copy-done.1) | copy-start | bytes 983044
Sparse Core Ops, SparseCore 0:
  9.6 59.9 all-gather.1
  129.3 18.1 reduce-scatter.6
  150.0 21.4 reduce-scatter.4
where the time goes:
time: 181 us
  blocking collectives  79.7 us (44%)
  waiting for transfers between devices  41.3 us (23%)
  matrix products  22.8 us (13%)
  between operations  14.4 us (8%)
  local copies, waits for them, and re-layouts  12 us (7%)
  starting transfers between devices  5.28 us (3%)
  other arithmetic  4.77 us (3%)
    psum x1, blocking collectives, body(): total_one, total_two = lax.psum((sum_one, sum_two), ('row', 'col'))  35.7 us
    reduce_scatter x1, waiting for transfers between devices, body(): lax.psum_scatter(scaled_sum.astype(jnp.bfloat16), 'col', scatter_dimensio...  23 us
    unnamed x4, waiting for transfers between devices  16.5 us
    all_gather x1, blocking collectives, body(): query_all = lax.all_gather(query_rows, 'col', axis=1, tiled=True)  15.4 us
    dot_general x9, matrix products, body(): jnp.dot(padded[:, down:down + rows, across:across + columns, :], piece[do...  13.7 us
    all_gather x1, blocking collectives, body(): lax.all_gather(stale_k, 'row', axis=1, tiled=True)  10.8 us
    all_gather x1, blocking collectives, body(): lax.all_gather(stale_v, 'row', axis=1, tiled=True)  9.07 us
    pmax x1, blocking collectives, body(): top = lax.pmax(raised.astype(jnp.bfloat16), 'col').astype(raised.dtype)  8.73 us
  transfers between devices with their start and end apart: 7, of which 3 were waited for; matrix products, arithmetic and copies ran while one was open for 4% of the time, Pallas kernels for 0%

commit v1 on v0

v1 whole, which is shorter than its diff:
```python
import functools

import jax
import jax.numpy as jnp
from jax import lax
from jax.experimental import pallas as pl
from jax.experimental.pallas import tpu as pltpu
from jax.sharding import PartitionSpec as P

HD = 64
GROUPS = 32
PAIR = 2
MESH = pl.DeviceIdType.MESH
F32 = jnp.float32
BF16 = jnp.bfloat16


def time_features(timestep, width):
    half = width // 2
    freqs = jnp.exp(-jnp.log(10000.0) * jnp.arange(half, dtype=jnp.float32) / half)
    angles = timestep.astype(jnp.float32)[:, None] * freqs[None, :]
    return jnp.concatenate([jnp.cos(angles), jnp.sin(angles)], axis=1)


def group_total(sums, size):
    width = sums.shape[1]
    lane = lax.broadcasted_iota(jnp.int32, sums.shape, 1)

    def window(x, sign):
        parts, total, offset = {1: x}, None, 0
        step = 1
        while step * 2 <= size:
            last = parts[step]
            parts[step * 2] = last + pltpu.roll(last, (sign * step) % width, 1)
            step *= 2
        for step in sorted(parts, reverse=True):
            if size & step:
                piece = parts[step]
                if offset:
                    piece = pltpu.roll(piece, (sign * offset) % width, 1)
                total = piece if total is None else total + piece
                offset += step
        return total

    ends = jnp.where(lax.rem(lane, size) == size - 1, window(sums, 1), 0.0)
    return window(ends, -1)


def kernel(
    dims,
    lat_ref,
    edge_ref,
    tb_ref,
    gg_ref,
    gb_ref,
    lg_ref,
    cw_hbm,
    qw_hbm,
    kw_hbm,
    vw_hbm,
    ow_hbm,
    sk_hbm,
    sv_hbm,
    mixed_ref,
    fk_ref,
    fv_ref,
    band,
    halo,
    acts,
    raw,
    cw,
    qkvw,
    ow,
    stats,
    hsend,
    hbuf,
    hfull,
    kbuf,
    vbuf,
    qown,
    qin,
    own_o,
    own_s,
    out_o,
    out_s,
    in_o,
    in_s,
    attn,
    load_sem,
    row_send,
    row_recv,
    col_send,
    col_recv,
    edge_send,
    edge_recv,
    fwd_send,
    fwd_recv,
    x_send,
    x_recv,
):
    R, C, NX, rows, cols, channels, inner, count_all = dims
    span = rows * cols
    wide = channels // R
    nb = 2
    me = lax.axis_index("row")
    mc = lax.axis_index("col")

    def remote(src, dst, send, recv, **where):
        return pltpu.make_async_remote_copy(
            src_ref=src, dst_ref=dst, send_sem=send, recv_sem=recv, device_id=where, device_id_type=MESH
        )

    loads = [
        pltpu.make_async_copy(cw_hbm, cw, load_sem.at[0]),
        pltpu.make_async_copy(qw_hbm, qkvw.at[:, 0:inner], load_sem.at[1]),
        pltpu.make_async_copy(kw_hbm, qkvw.at[:, inner : 2 * inner], load_sem.at[2]),
        pltpu.make_async_copy(vw_hbm, qkvw.at[:, 2 * inner : 3 * inner], load_sem.at[3]),
        pltpu.make_async_copy(ow_hbm, ow, load_sem.at[4]),
        pltpu.make_async_copy(sk_hbm, kbuf.at[:, 0:span], load_sem.at[5]),
        pltpu.make_async_copy(sv_hbm, vbuf.at[:, 0:span], load_sem.at[6]),
    ]
    for load in loads:
        load.start()

    barrier = pltpu.get_barrier_semaphore()
    for d in range(1, R):
        pl.semaphore_signal(barrier, inc=1, device_id={"row": lax.rem(me + d, R)}, device_id_type=MESH)
    for d in range(1, C):
        pl.semaphore_signal(barrier, inc=1, device_id={"col": lax.rem(mc + d, C)}, device_id_type=MESH)
    pl.semaphore_wait(barrier, R - 1 + C - 1)

    to_right = remote(edge_ref.at[0], halo.at[me, 0], edge_send.at[0], edge_recv.at[0], col=lax.rem(mc + 1, C))
    to_left = remote(edge_ref.at[1], halo.at[me, 1], edge_send.at[1], edge_recv.at[1], col=lax.rem(mc + C - 1, C))

    @pl.when(mc < C - 1)
    def _():
        to_right.start()

    @pl.when(mc > 0)
    def _():
        to_left.start()

    lat_out = []
    for d in range(1, R):
        copy = remote(lat_ref, band.at[me], row_send.at[0, d], row_recv.at[0, d], row=lax.rem(me + d, R))
        copy.start()
        lat_out.append(copy)
    band[me] = lat_ref[...]

    @pl.when(mc == 0)
    def _():
        halo[me, 0] = jnp.zeros(halo.shape[2:], F32)

    @pl.when(mc == C - 1)
    def _():
        halo[me, 1] = jnp.zeros(halo.shape[2:], F32)

    @pl.when(mc > 0)
    def _():
        to_right.wait_recv()

    @pl.when(mc < C - 1)
    def _():
        to_left.wait_recv()

    halo_out = []
    for d in range(1, R):
        copy = remote(halo.at[me], halo.at[me], row_send.at[1, d], row_recv.at[1, d], row=lax.rem(me + d, R))
        copy.start()
        halo_out.append(copy)
    for copy in lat_out:
        copy.wait_recv()

    one = [jnp.zeros((cols, channels), F32) for _ in range(nb)]
    two = [jnp.zeros((cols, channels), F32) for _ in range(nb)]
    for r in range(R):
        halves = []
        for b in range(nb):
            x = band[r, b].astype(F32)
            one[b] = one[b] + jnp.sum(x, axis=0)
            two[b] = two[b] + jnp.sum(x * x, axis=0)
            halves.append(x)
        raw[r * rows : (r + 1) * rows] = jnp.concatenate(halves, axis=1).astype(BF16)
    rows_of = [jnp.sum(x, axis=0, keepdims=True) for x in one + two]
    stats[0] = jnp.concatenate(rows_of + rows_of, axis=0)
    stat_out = []
    for d in range(1, C):
        copy = remote(
            stats.at[0], stats.at[C - d], col_send.at[0, d], col_recv.at[0, d], col=lax.rem(mc + d, C)
        )
        copy.start()
        stat_out.append(copy)
    loads[5].wait()
    loads[6].wait()
    stale_out = []
    for d in range(1, C):
        for n, buf in ((1, kbuf), (2, vbuf)):
            copy = remote(
                buf.at[:, 0:span],
                buf.at[:, (C - d) * span : (C - d + 1) * span],
                col_send.at[n, d],
                col_recv.at[n, d],
                col=lax.rem(mc + d, C),
            )
            copy.start()
            stale_out.append(copy)
    pick = (
        lax.broadcasted_iota(jnp.int32, (channels, wide), 0)
        == lax.broadcasted_iota(jnp.int32, (channels, wide), 1) + me * wide
    )
    acc = jnp.dot(
        raw[...].reshape(R * rows * nb * cols, channels),
        jnp.where(pick, 1.0, 0.0).astype(BF16),
        preferred_element_type=F32,
    )
    for copy in stat_out:
        copy.wait_recv()
    total = stats[0]
    for d in range(1, C):
        total = total + stats[d]
    total = group_total(total, channels // GROUPS) * (1.0 / count_all)
    mean = [total[b : b + 1] for b in range(nb)]
    scale = [lax.rsqrt(total[nb + b : nb + b + 1] - mean[b] * mean[b] + 1e-05) * gg_ref[...] for b in range(nb)]
    bias = gb_ref[...]

    def activate(x, b):
        y = (x - mean[b]) * scale[b] + bias
        return y * jax.nn.sigmoid(y)

    for copy in halo_out:
        copy.wait_recv()
    place = lax.broadcasted_iota(jnp.int32, (rows, cols, channels), 1)
    for t in range(3):
        acts[t, 0] = jnp.zeros(acts.shape[2:], BF16)
        acts[t, R * rows + 1] = jnp.zeros(acts.shape[2:], BF16)
    for r in range(R):
        tap = [[], [], []]
        for b in range(nb):
            a = activate(band[r, b].astype(F32), b)
            left = jnp.where(mc > 0, activate(halo[r, 0, b], b), 0.0)
            right = jnp.where(mc < C - 1, activate(halo[r, 1, b], b), 0.0)
            tap[0].append(jnp.where(place == 0, left, pltpu.roll(a, 1, 1)))
            tap[1].append(a)
            tap[2].append(jnp.where(place == cols - 1, right, pltpu.roll(a, cols - 1, 1)))
        for t in range(3):
            acts[t, 1 + r * rows : 1 + (r + 1) * rows] = jnp.concatenate(tap[t], axis=1).astype(BF16)
    loads[0].wait()
    for across in range(3):
        for down in range(3):
            acc = acc + jnp.dot(
                acts[across, down : down + R * rows].reshape(R * rows * nb * cols, channels),
                cw[down, across],
                preferred_element_type=F32,
            )
    hid = acc.reshape(R * rows, nb * cols, wide) + tb_ref[...][None]
    hsend[...] = hid.reshape(R, nb * span, wide).astype(BF16)
    h_out = []
    for d in range(1, R):
        to = lax.rem(me + d, R)
        copy = remote(hsend.at[to], hbuf.at[me], row_send.at[2, d], row_recv.at[2, d], row=to)
        copy.start()
        h_out.append(copy)
    hbuf[me] = hsend[me]
    for copy in stale_out:
        copy.wait_recv()
    mate = me + 1 - 2 * lax.rem(me, PAIR)
    forwards = []
    for n, buf in enumerate((kbuf, vbuf)):
        copy = remote(
            buf.at[:, 0 : C * span], buf.at[:, C * span : 2 * C * span], fwd_send.at[n], fwd_recv.at[n], row=mate
        )
        copy.start()
        forwards.append(copy)
    for copy in h_out:
        copy.wait_recv()
    h = jnp.concatenate([hbuf[r].astype(F32) for r in range(R)], axis=1)
    hfull[...] = h
    centre = h - jnp.mean(h, axis=1, keepdims=True)
    spread = jnp.mean(centre * centre, axis=1, keepdims=True)
    normed = (centre * lax.rsqrt(spread + 1e-05) * lg_ref[...]).astype(BF16)
    for n in (1, 2, 3):
        loads[n].wait()
    qkv = jnp.dot(normed, qkvw[...], preferred_element_type=F32).reshape(rows, nb, cols, 3 * inner)
    for b in range(nb):
        part = qkv[:, b].reshape(span, 3 * inner)
        qown[b] = (part[:, 0:inner] * (1.0 / HD**0.5)).astype(BF16)
        k = part[:, inner : 2 * inner].astype(BF16)
        v = part[:, 2 * inner :].astype(BF16)
        kbuf[b, 2 * C * span :] = k
        vbuf[b, 2 * C * span :] = v
        fk_ref[b] = k
        fv_ref[b] = v
    q_out = []
    for d in range(1, NX):
        copy = remote(
            qown, qin.at[NX - d], x_send.at[0, d], x_recv.at[0, d], row=lax.rem(me + d * PAIR, R)
        )
        copy.start()
        q_out.append(copy)
    for copy in forwards:
        copy.wait_recv()

    half = lax.broadcasted_iota(jnp.int32, (span, 2 * HD), 1) < HD
    lanes = lax.broadcasted_iota(jnp.int32, (span, 128), 1)
    zero = jnp.zeros((span, 2 * HD), BF16)

    def attend(q, b, start, o_store):
        held = jnp.zeros((span, 128), F32)
        for pair in range(inner // (2 * HD)):
            at = slice(pair * 2 * HD, (pair + 1) * 2 * HD)
            q2 = q[:, at]
            q2 = jnp.concatenate([jnp.where(half, q2, zero), jnp.where(half, zero, q2)], axis=0)
            s = lax.dot_general(
                q2, kbuf[b, start : start + 2 * C * span, at], (((1,), (1,)), ((), ())), preferred_element_type=F32
            )
            m = jnp.max(s, axis=1, keepdims=True)
            p = jnp.exp(s - m)
            l = jnp.sum(p, axis=1, keepdims=True)
            o = jnp.dot(p.astype(BF16), vbuf[b, start : start + 2 * C * span, at], preferred_element_type=F32)
            o_store(at, jnp.where(half, o[:span], o[span:]))
            for n in range(2):
                held = jnp.where(lanes == pair * 2 + n, m[n * span : (n + 1) * span], held)
                held = jnp.where(lanes == 64 + pair * 2 + n, l[n * span : (n + 1) * span], held)
        return held

    for b in range(nb):

        def keep(at, o, b=b):
            own_o[b, :, at] = o

        own_s[b] = attend(qown[b], b, span, keep)

    back = []
    for d in range(1, NX):
        q_out[NX - 1 - d].wait_recv()
        for b in range(nb):

            def give(at, o, b=b, d=d):
                out_o[d, b, :, at] = o.astype(BF16)

            out_s[d, b] = attend(qin[d, b], b, 0, give)
        to = lax.rem(me + d * PAIR, R)
        for n, src, dst in ((1, out_o, in_o), (2, out_s, in_s)):
            copy = remote(src.at[d], dst.at[NX - d], x_send.at[n, d], x_recv.at[n, d], row=to)
            copy.start()
            back.append(copy)
    for copy in back:
        copy.wait_recv()
    loads[4].wait()
    for b in range(nb):
        for pair in range(inner // (2 * HD)):
            at = slice(pair * 2 * HD, (pair + 1) * 2 * HD)

            def spread_of(held, base):
                one_of = held[:, base + pair * 2 : base + pair * 2 + 1]
                two_of = held[:, base + pair * 2 + 1 : base + pair * 2 + 2]
                return jnp.where(half, one_of, two_of)

            helds = [own_s[b]] + [in_s[d, b] for d in range(1, NX)]
            sums = [own_o[b, :, at]] + [in_o[d, b, :, at].astype(F32) for d in range(1, NX)]
            peaks = [spread_of(held, 0) for held in helds]
            top = functools.reduce(jnp.maximum, peaks)
            num, den = 0.0, 0.0
            for held, o, peak in zip(helds, sums, peaks):
                factor = jnp.exp(peak - top)
                num = num + o * factor
                den = den + spread_of(held, 64) * factor
            attn[b, :, at] = (num / den).astype(BF16)
        hb = hfull[...].reshape(rows, nb, cols, channels)[:, b].reshape(span, channels)
        mixed_ref[b] = (hb + jnp.dot(attn[b], ow[...], preferred_element_type=F32)).astype(BF16)

    @pl.when(mc < C - 1)
    def _():
        to_right.wait_send()

    @pl.when(mc > 0)
    def _():
        to_left.wait_send()

    for copy in lat_out + halo_out + stat_out + stale_out + h_out + forwards + q_out + back:
        copy.wait_send()


def body(
    latent,
    timestep,
    gn_gain,
    gn_bias,
    conv_weight,
    conv_bias,
    time_weight,
    ln_gain,
    q_weight,
    k_weight,
    v_weight,
    out_weight,
    stale_keys,
    stale_values,
):
    batch, rows, cols, channels = latent.shape
    inner = q_weight.shape[1]
    R, C = lax.axis_size("row"), lax.axis_size("col")
    NX = R // PAIR
    span = rows * cols
    wide = conv_weight.shape[3]
    count_all = span * R * C * (channels // GROUPS)
    me = lax.axis_index("row")
    emb = jax.nn.silu(time_features(timestep, time_weight.shape[0])).astype(BF16)
    temb = jnp.dot(emb, time_weight, preferred_element_type=F32) + conv_bias
    temb = lax.dynamic_slice_in_dim(temb, me * wide, wide, 1)
    temb = jnp.repeat(temb, cols, axis=0)
    edges = jnp.stack([latent[:, :, cols - 1], latent[:, :, 0]]).astype(F32)[:, :, :, None, :]
    vm = pl.BlockSpec(memory_space=pltpu.VMEM)
    hbm = pl.BlockSpec(memory_space=pl.ANY)
    dma = pltpu.SemaphoreType.DMA
    mixed, fresh_k, fresh_v = pl.pallas_call(
        functools.partial(kernel, (R, C, NX, rows, cols, channels, inner, count_all)),
        out_shape=(
            jax.ShapeDtypeStruct((batch, span, channels), BF16),
            jax.ShapeDtypeStruct((batch, span, inner), BF16),
            jax.ShapeDtypeStruct((batch, span, inner), BF16),
        ),
        in_specs=[vm] * 6 + [hbm] * 7,
        out_specs=(vm, vm, vm),
        scratch_shapes=[
            pltpu.VMEM((R, batch, rows, cols, channels), BF16),
            pltpu.VMEM((R, 2, batch, rows, 1, channels), F32),
            pltpu.VMEM((3, R * rows + 2, batch * cols, channels), BF16),
            pltpu.VMEM((R * rows, batch * cols, channels), BF16),
            pltpu.VMEM(conv_weight.shape, BF16),
            pltpu.VMEM((channels, 3 * inner), BF16),
            pltpu.VMEM((inner, channels), BF16),
            pltpu.VMEM((C, 8, channels), F32),
            pltpu.VMEM((R, batch * span, wide), BF16),
            pltpu.VMEM((R, batch * span, wide), BF16),
            pltpu.VMEM((batch * span, channels), F32),
            pltpu.VMEM((batch, (2 * C + 1) * span, inner), BF16),
            pltpu.VMEM((batch, (2 * C + 1) * span, inner), BF16),
            pltpu.VMEM((batch, span, inner), BF16),
            pltpu.VMEM((NX, batch, span, inner), BF16),
            pltpu.VMEM((batch, span, inner), F32),
            pltpu.VMEM((batch, span, 128), F32),
            pltpu.VMEM((NX, batch, span, inner), BF16),
            pltpu.VMEM((NX, batch, span, 128), F32),
            pltpu.VMEM((NX, batch, span, inner), BF16),
            pltpu.VMEM((NX, batch, span, 128), F32),
            pltpu.VMEM((batch, span, inner), BF16),
            dma((7,)),
            dma((3, R)),
            dma((3, R)),
            dma((3, C)),
            dma((3, C)),
            dma((2,)),
            dma((2,)),
            dma((2,)),
            dma((2,)),
            dma((3, NX)),
            dma((3, NX)),
        ],
        compiler_params=pltpu.CompilerParams(
            collective_id=0, has_side_effects=True, vmem_limit_bytes=56 * 1024 * 1024
        ),
    )(
        latent,
        edges,
        temb,
        gn_gain.reshape(1, channels),
        gn_bias.reshape(1, channels),
        ln_gain.reshape(1, channels),
        conv_weight,
        q_weight,
        k_weight,
        v_weight,
        out_weight,
        stale_keys.reshape(batch, span, inner),
        stale_values.reshape(batch, span, inner),
    )
    return (
        mixed.reshape(batch, rows, cols, channels),
        fresh_k.reshape(batch, rows, cols, inner),
        fresh_v.reshape(batch, rows, cols, inner),
    )


def solution(mesh):
    placed = (
        P("parts", "row", "col", None),
        P("parts"),
        P(),
        P(),
        P(None, None, None, "row"),
        P(),
        P(),
        P(),
        P(),
        P(),
        P(),
        P(),
        P("parts", "row", "col", None),
        P("parts", "row", "col", None),
    )
    return jax.shard_map(
        body,
        mesh=mesh,
        in_specs=placed,
        out_specs=(
            P("parts", "row", "col", None),
            P("parts", "row", "col", None),
            P("parts", "row", "col", None),
        ),
        check_vma=False,
    )
```

time: 181 us -> 64.2 us (0.35)
  blocking collectives: 79.7 us -> 0 us
  Pallas kernels: 0 us -> 45.1 us
  waiting for transfers between devices: 41.3 us -> 0 us
  matrix products: 22.8 us -> 0.21 us
  between operations: 14.4 us -> 0.7 us
  starting transfers between devices: 5.28 us -> 0 us
  local copies, waits for them, and re-layouts: 12 us -> 16.1 us
  other arithmetic: 4.77 us -> 1.66 us
    pallas_call x0 -> x1, Pallas kernels: none -> 45.1 us  [body(): pl.pallas_call(functools.partial(kernel, (R, C, NX, rows, cols, channels,...]
    psum x1 -> x0, blocking collectives: 35.7 us -> none  [body(): total_one, total_two = lax.psum((sum_one, sum_two), ('row', 'col'))]
    all_gather x3 -> x0, blocking collectives: 35.2 us -> none  [the longest x1 15.4 us: body(): query_all = lax.all_gather(query_rows, 'col', axis=1, tiled=True)]
    reduce_scatter x1 -> x0, waiting for transfers between devices: 23 us -> none  [body(): lax.psum_scatter(scaled_sum.astype(jnp.bfloat16), 'col', scatter_dimensio...]
    dot_general x20 -> x1, matrix products: 22.8 us -> 0.21 us  [body(): temb = jnp.dot(emb, time_weight, preferred_element_type=F32) + conv_bias]
    unnamed x4 -> x0, waiting for transfers between devices: 16.5 us -> none
    pmax x1 -> x0, blocking collectives: 8.73 us -> none  [body(): top = lax.pmax(raised.astype(jnp.bfloat16), 'col').astype(raised.dtype)]
    unnamed x41 -> x6, local copies, waits for them, and re-layouts: 4.5 us -> 9.77 us
  transfers between devices with their start and end apart: 7 -> 0, of which waited for: 3 -> 0; matrix products, arithmetic and copies ran while one was open for 4% -> 0% of each run, Pallas kernels for 0% -> 0%
where the time goes in v1:
time: 64.2 us; the launch traced here: 63.7 us
  Pallas kernels  45.1 us (70%)
  local copies, waits for them, and re-layouts  16.1 us (25%)
  other arithmetic  1.66 us (3%)
  between operations  0.7 us (1%)
    pallas_call x1, Pallas kernels, body(): pl.pallas_call(functools.partial(kernel, (R, C, NX, rows, cols, channels,...  45.1 us
    unnamed x6, local copies, waits for them, and re-layouts  9.77 us

profile of v1, /device:TPU:0, one launch (start us, length us, event | category | flops | bytes accessed | tf_op | source)
XLA Modules:
  0.0 63.7 jit_solution(13503613351923751095)
XLA Ops:
  0.6 0.0 copy-start
  0.7 0.7 %convert_element_type.17 = f32[2]{0:T(128)S(1)} convert(s32[2]{0:T(128)} %param.15) | non-fusion elementwise | flops 2 | bytes 16 | tf_op jit(solution)/shard_map/convert_element_type | solution.py:21
  1.4 0.8 %dynamic-slice = f32[160]{0:T(256)S(1)} dynamic-slice(f32[640]{0:T(1024)} %param.19, s32[]{:T(128)S(6)} %select_n.3), dynamic_slice_sizes={160} | dynamic-slice | bytes 1284 | tf_op jit(solution)/shard_map/dynamic_slice | solution.py:410
  2.1 1.3 %reshape.72.gg_ref = f32[1,640]{1,0:T(1,128)} reshape(f32[640]{0:T(1024)} %param.16) | data formatting | bytes 5120 | tf_op jit(solution)/shard_map/reshape | solution.py:467
  3.4 1.3 %reshape.73.gb_ref = f32[1,640]{1,0:T(1,128)} reshape(f32[640]{0:T(1024)} %param.17) | data formatting | bytes 5120 | tf_op jit(solution)/shard_map/reshape | solution.py:468
  4.7 1.3 %reshape.74.lg_ref = f32[1,640]{1,0:T(1,128)} reshape(f32[640]{0:T(1024)} %param.21) | data formatting | bytes 5120 | tf_op jit(solution)/shard_map/reshape | solution.py:469
  6.0 0.1 multiply_cosine_fusion
  6.1 0.0 copy-done
  6.1 0.2 fusion.1
  6.3 0.1 dynamic-slice_add_fusion
  6.4 0.6 broadcast_bitcast_fusion.tb_ref
  7.0 1.1 %fusion.6 = (bf16[2,8,1,640]{3,2,1,0:T(2,128)(2,1)S(1)}, bf16[2,8,1,640]{3,2,1,0:T(2,128)(2,1)S(1)}) fusion(bf16[2,8,8,640]{3,2,1,0:T(8,128)(2,1)} %lat_ref.1), kind=kLoop, calls=%fused_computation.15 | loop fusion | bytes 81920 | tf_op jit(solution)/shard_map/slice | solution.py:412
  8.2 0.7 %maximum_convert_fusion.edge_ref = f32[2,2,8,1,640]{4,3,2,1,0:T(1,128)} fusion(bf16[1,2,8,1,640]{4,3,2,1,0:T(2,128)(2,1)S(1)} %copy.23, bf16[1,2,8,1,640]{4,3,2,1,0:T(2,128)(2,1)S(1)} %copy.22), kind=kLoop, calls=%fused_computation | loop fusion | flops 40960 | bytes 122880 | tf_op jit(solution)/shard_map/convert_element_type | solution.py:412
  8.9 5.1 %copy.24.cw_hbm = bf16[3,3,640,160]{3,2,1,0:T(8,128)(2,1)} copy(bf16[3,3,640,160]{2,3,1,0:T(8,128)(2,1)} %param.18) | data formatting | bytes 3686400 | tf_op args[4]
  14.0 45.1 %shard_map.157 = (bf16[2,64,640]{2,1,0:T(8,128)(2,1)}, bf16[2,64,384]{2,1,0:T(8,128)(2,1)}, bf16[2,64,384]{2,1,0:T(8,128)(2,1)}) custom-call(bf16[2,8,8,640]{3,2,1,0:T(8,128)(2,1)} %lat_ref.1, f32[2,2,8,1,640]{4,3,2,1,0:T(1,128)} %maximum_convert_fusion.edge_ref, f32[16,160]{1,0:T(8,128)} %broadcast_bitcast_fusion.tb_ref, f32[1,640]{1,0:T(1,128)} %reshape.72.gg_ref, ...), custom_call_target="tpu_custom_call" | custom-call | tf_op jit(solution)/shard_map/pallas_call | solution.py:416
  59.1 1.6 %copy.32 = bf16[2,8,8,640]{3,2,1,0:T(8,128)(2,1)} copy(bf16[2,8,8,640]{3,2,1,0:T(8,128)(2,1)} %bitcast.12) | data formatting | bytes 327680
  60.7 1.5 %copy.33 = bf16[2,8,8,384]{3,2,1,0:T(8,128)(2,1)} copy(bf16[2,8,8,384]{3,2,1,0:T(8,128)(2,1)} %bitcast.14) | data formatting | bytes 196608
  62.2 1.5 %copy.34 = bf16[2,8,8,384]{3,2,1,0:T(8,128)(2,1)} copy(bf16[2,8,8,384]{3,2,1,0:T(8,128)(2,1)} %bitcast.13) | data formatting | bytes 196608
  (4 shorter events, 0.1 us)
Async XLA Ops:
  0.6 5.5 %copy-start = (bf16[320,640]{1,0:T(8,128)(2,1)S(1)}, bf16[320,640]{1,0:T(8,128)(2,1)}, u32[]{:S(2)}) copy-start(bf16[320,640]{1,0:T(8,128)(2,1)} %param.20) | copy-start | bytes 1228804

commit v2 on v1

--- a/solution.py
+++ b/solution.py
@@ -10,16 +10,10 @@
 HD = 64
 GROUPS = 32
 PAIR = 2
+EARLY = True
 MESH = pl.DeviceIdType.MESH
 F32 = jnp.float32
 BF16 = jnp.bfloat16
-
-
-def time_features(timestep, width):
-    half = width // 2
-    freqs = jnp.exp(-jnp.log(10000.0) * jnp.arange(half, dtype=jnp.float32) / half)
-    angles = timestep.astype(jnp.float32)[:, None] * freqs[None, :]
-    return jnp.concatenate([jnp.cos(angles), jnp.sin(angles)], axis=1)
 
 
 def group_total(sums, size):
@@ -46,14 +40,38 @@
     return window(ends, -1)
 
 
+def send_stale(go, kbuf, vbuf, span, C, mc, col_send, col_recv):
+    return [
+        go(
+            buf.at[:, 0:span],
+            buf.at[:, (C - d) * span : (C - d + 1) * span],
+            col_send.at[n, d],
+            col_recv.at[n, d],
+            col=lax.rem(mc + d, C),
+        )
+        for d in range(1, C)
+        for n, buf in ((1, kbuf), (2, vbuf))
+    ]
+
+
+def finish(a, b, c, x, y, z, sem):
+    copies = [pltpu.make_async_copy(s, d, sem.at[n]) for n, (s, d) in enumerate(((a, x), (b, y), (c, z)))]
+    for copy in copies:
+        copy.start()
+    for copy in copies:
+        copy.wait()
+
+
 def kernel(
     dims,
-    lat_ref,
-    edge_ref,
-    tb_ref,
+    t_ref,
+    freq_ref,
     gg_ref,
     gb_ref,
     lg_ref,
+    bias_ref,
+    lat_hbm,
+    tw_hbm,
     cw_hbm,
     qw_hbm,
     kw_hbm,
@@ -65,7 +83,9 @@
     fk_ref,
     fv_ref,
     band,
+    edges,
     halo,
+    tw,
     acts,
     raw,
     cw,
@@ -118,19 +138,36 @@
         pltpu.make_async_copy(ow_hbm, ow, load_sem.at[4]),
         pltpu.make_async_copy(sk_hbm, kbuf.at[:, 0:span], load_sem.at[5]),
         pltpu.make_async_copy(sv_hbm, vbuf.at[:, 0:span], load_sem.at[6]),
+        pltpu.make_async_copy(tw_hbm, tw, load_sem.at[7]),
     ]
-    for load in loads:
-        load.start()
+    own_load = pltpu.make_async_copy(lat_hbm, band.at[me], load_sem.at[8])
+    own_load.start()
 
     barrier = pltpu.get_barrier_semaphore()
     for d in range(1, R):
         pl.semaphore_signal(barrier, inc=1, device_id={"row": lax.rem(me + d, R)}, device_id_type=MESH)
     for d in range(1, C):
         pl.semaphore_signal(barrier, inc=1, device_id={"col": lax.rem(mc + d, C)}, device_id_type=MESH)
+    for n in (5, 6, 7, 0, 1, 2, 3, 4):
+        loads[n].start()
+    own_load.wait()
+    for b in range(nb):
+        x = band[me, b].astype(F32)
+        edges[0, b] = x[:, cols - 1 :, :]
+        edges[1, b] = x[:, 0:1, :]
+    mate = me + 1 - 2 * lax.rem(me, PAIR)
+    started = []
+
+    def go(src, dst, send, recv, **where):
+        copy = remote(src, dst, send, recv, **where)
+        copy.start()
+        started.append(copy)
+        return copy
+
     pl.semaphore_wait(barrier, R - 1 + C - 1)
 
-    to_right = remote(edge_ref.at[0], halo.at[me, 0], edge_send.at[0], edge_recv.at[0], col=lax.rem(mc + 1, C))
-    to_left = remote(edge_ref.at[1], halo.at[me, 1], edge_send.at[1], edge_recv.at[1], col=lax.rem(mc + C - 1, C))
+    to_right = remote(edges.at[0], halo.at[me, 0], edge_send.at[0], edge_recv.at[0], col=lax.rem(mc + 1, C))
+    to_left = remote(edges.at[1], halo.at[me, 1], edge_send.at[1], edge_recv.at[1], col=lax.rem(mc + C - 1, C))
 
     @pl.when(mc < C - 1)
     def _():
@@ -140,12 +177,25 @@
     def _():
         to_left.start()
 
-    lat_out = []
-    for d in range(1, R):
-        copy = remote(lat_ref, band.at[me], row_send.at[0, d], row_recv.at[0, d], row=lax.rem(me + d, R))
-        copy.start()
-        lat_out.append(copy)
-    band[me] = lat_ref[...]
+    def spread(ref, n):
+        cross = [
+            go(ref, ref, row_send.at[n, k], row_recv.at[n, k], row=lax.rem(me + k * PAIR, R)) for k in range(1, NX)
+        ]
+        return [go(ref, ref, row_send.at[n, 0], row_recv.at[n, 0], row=mate)], cross
+
+    def relay(cross, at, n):
+        handed = []
+        for k in range(1, NX):
+            cross[k - 1].wait_recv()
+            ref = at(lax.rem(me + R - k * PAIR, R))
+            handed.append(go(ref, ref, row_send.at[n, NX - 1 + k], row_recv.at[n, NX - 1 + k], row=mate))
+        return handed
+
+    lat_out = [spread(band.at[me, b], b) for b in range(nb)]
+    if EARLY:
+        loads[5].wait()
+        loads[6].wait()
+        stale_out = send_stale(go, kbuf, vbuf, span, C, mc, col_send, col_recv)
 
     @pl.when(mc == 0)
     def _():
@@ -163,12 +213,27 @@
     def _():
         to_left.wait_recv()
 
-    halo_out = []
-    for d in range(1, R):
-        copy = remote(halo.at[me], halo.at[me], row_send.at[1, d], row_recv.at[1, d], row=lax.rem(me + d, R))
-        copy.start()
-        halo_out.append(copy)
-    for copy in lat_out:
+    halo_out = spread(halo.at[me], nb)
+
+    half_t = freq_ref.shape[1]
+    line = lax.broadcasted_iota(jnp.int32, (nb * cols, half_t), 0)
+    when = jnp.where(line < cols, t_ref[0], t_ref[1]).astype(F32)
+    angles = when * freq_ref[...]
+    loads[7].wait()
+    temb = jnp.dot(
+        jax.nn.silu(jnp.cos(angles)).astype(BF16), tw[0:half_t, :], preferred_element_type=F32
+    ) + jnp.dot(jax.nn.silu(jnp.sin(angles)).astype(BF16), tw[half_t:, :], preferred_element_type=F32)
+    temb = temb + bias_ref[...].reshape(1, channels)
+    tb = temb[:, 0:wide]
+    for r in range(1, R):
+        tb = jnp.where(me == r, temb[:, r * wide : (r + 1) * wide], tb)
+
+    handed = []
+    for b in range(nb):
+        handed += relay(lat_out[b][1], lambda p, b=b: band.at[p, b], b)
+    for b in range(nb):
+        lat_out[b][0][0].wait_recv()
+    for copy in handed:
         copy.wait_recv()
 
     one = [jnp.zeros((cols, channels), F32) for _ in range(nb)]
@@ -183,27 +248,15 @@
         raw[r * rows : (r + 1) * rows] = jnp.concatenate(halves, axis=1).astype(BF16)
     rows_of = [jnp.sum(x, axis=0, keepdims=True) for x in one + two]
     stats[0] = jnp.concatenate(rows_of + rows_of, axis=0)
-    stat_out = []
-    for d in range(1, C):
-        copy = remote(
-            stats.at[0], stats.at[C - d], col_send.at[0, d], col_recv.at[0, d], col=lax.rem(mc + d, C)
-        )
-        copy.start()
-        stat_out.append(copy)
-    loads[5].wait()
-    loads[6].wait()
-    stale_out = []
-    for d in range(1, C):
-        for n, buf in ((1, kbuf), (2, vbuf)):
-            copy = remote(
-                buf.at[:, 0:span],
-                buf.at[:, (C - d) * span : (C - d + 1) * span],
-                col_send.at[n, d],
-                col_recv.at[n, d],
-                col=lax.rem(mc + d, C),
-            )
-            copy.start()
-            stale_out.append(copy)
+    stat_out = [
+        go(stats.at[0], stats.at[C - d], col_send.at[0, d], col_recv.at[0, d], col=lax.rem(mc + d, C))
+        for d in range(1, C)
+    ]
+    handed = relay(halo_out[1], lambda p: halo.at[p], nb)
+    if not EARLY:
+        loads[5].wait()
+        loads[6].wait()
+        stale_out = send_stale(go, kbuf, vbuf, span, C, mc, col_send, col_recv)
     pick = (
         lax.broadcasted_iota(jnp.int32, (channels, wide), 0)
         == lax.broadcasted_iota(jnp.int32, (channels, wide), 1) + me * wide
@@ -220,14 +273,14 @@
         total = total + stats[d]
     total = group_total(total, channels // GROUPS) * (1.0 / count_all)
     mean = [total[b : b + 1] for b in range(nb)]
-    scale = [lax.rsqrt(total[nb + b : nb + b + 1] - mean[b] * mean[b] + 1e-05) * gg_ref[...] for b in range(nb)]
-    bias = gb_ref[...]
+    scale = [lax.rsqrt(total[nb + b : nb + b + 1] - mean[b] * mean[b] + 1e-05) * gg_ref[...].reshape(1, channels) for b in range(nb)]
+    bias = gb_ref[...].reshape(1, channels)
 
     def activate(x, b):
         y = (x - mean[b]) * scale[b] + bias
         return y * jax.nn.sigmoid(y)
 
-    for copy in halo_out:
+    for copy in halo_out[0] + handed:
         copy.wait_recv()
     place = lax.broadcasted_iota(jnp.int32, (rows, cols, channels), 1)
     for t in range(3):
@@ -247,37 +300,32 @@
     loads[0].wait()
     for across in range(3):
         for down in range(3):
-            acc = acc + jnp.dot(
+            acc = acc + lax.dot_general(
                 acts[across, down : down + R * rows].reshape(R * rows * nb * cols, channels),
                 cw[down, across],
+                (((1,), (1,)), ((), ())),
                 preferred_element_type=F32,
             )
-    hid = acc.reshape(R * rows, nb * cols, wide) + tb_ref[...][None]
+    hid = acc.reshape(R * rows, nb * cols, wide) + tb[None]
     hsend[...] = hid.reshape(R, nb * span, wide).astype(BF16)
     h_out = []
     for d in range(1, R):
         to = lax.rem(me + d, R)
-        copy = remote(hsend.at[to], hbuf.at[me], row_send.at[2, d], row_recv.at[2, d], row=to)
-        copy.start()
-        h_out.append(copy)
+        h_out.append(go(hsend.at[to], hbuf.at[me], row_send.at[nb + 1, d], row_recv.at[nb + 1, d], row=to))
     hbuf[me] = hsend[me]
     for copy in stale_out:
         copy.wait_recv()
-    mate = me + 1 - 2 * lax.rem(me, PAIR)
-    forwards = []
-    for n, buf in enumerate((kbuf, vbuf)):
-        copy = remote(
-            buf.at[:, 0 : C * span], buf.at[:, C * span : 2 * C * span], fwd_send.at[n], fwd_recv.at[n], row=mate
-        )
-        copy.start()
-        forwards.append(copy)
+    forwards = [
+        go(buf.at[:, 0 : C * span], buf.at[:, C * span : 2 * C * span], fwd_send.at[n], fwd_recv.at[n], row=mate)
+        for n, buf in enumerate((kbuf, vbuf))
+    ]
     for copy in h_out:
         copy.wait_recv()
     h = jnp.concatenate([hbuf[r].astype(F32) for r in range(R)], axis=1)
     hfull[...] = h
     centre = h - jnp.mean(h, axis=1, keepdims=True)
     spread = jnp.mean(centre * centre, axis=1, keepdims=True)
-    normed = (centre * lax.rsqrt(spread + 1e-05) * lg_ref[...]).astype(BF16)
+    normed = (centre * lax.rsqrt(spread + 1e-05) * lg_ref[...].reshape(1, channels)).astype(BF16)
     for n in (1, 2, 3):
         loads[n].wait()
     qkv = jnp.dot(normed, qkvw[...], preferred_element_type=F32).reshape(rows, nb, cols, 3 * inner)
@@ -290,13 +338,10 @@
         vbuf[b, 2 * C * span :] = v
         fk_ref[b] = k
         fv_ref[b] = v
-    q_out = []
-    for d in range(1, NX):
-        copy = remote(
-            qown, qin.at[NX - d], x_send.at[0, d], x_recv.at[0, d], row=lax.rem(me + d * PAIR, R)
-        )
-        copy.start()
-        q_out.append(copy)
+    q_out = [
+        go(qown, qin.at[NX - d], x_send.at[0, d], x_recv.at[0, d], row=lax.rem(me + d * PAIR, R))
+        for d in range(1, NX)
+    ]
     for copy in forwards:
         copy.wait_recv()
 
@@ -341,9 +386,7 @@
             out_s[d, b] = attend(qin[d, b], b, 0, give)
         to = lax.rem(me + d * PAIR, R)
         for n, src, dst in ((1, out_o, in_o), (2, out_s, in_s)):
-            copy = remote(src.at[d], dst.at[NX - d], x_send.at[n, d], x_recv.at[n, d], row=to)
-            copy.start()
-            back.append(copy)
+            back.append(go(src.at[d], dst.at[NX - d], x_send.at[n, d], x_recv.at[n, d], row=to))
     for copy in back:
         copy.wait_recv()
     loads[4].wait()
@@ -377,7 +420,7 @@
     def _():
         to_left.wait_send()
 
-    for copy in lat_out + halo_out + stat_out + stale_out + h_out + forwards + q_out + back:
+    for copy in started:
         copy.wait_send()
 
 
@@ -404,12 +447,8 @@
     span = rows * cols
     wide = conv_weight.shape[3]
     count_all = span * R * C * (channels // GROUPS)
-    me = lax.axis_index("row")
-    emb = jax.nn.silu(time_features(timestep, time_weight.shape[0])).astype(BF16)
-    temb = jnp.dot(emb, time_weight, preferred_element_type=F32) + conv_bias
-    temb = lax.dynamic_slice_in_dim(temb, me * wide, wide, 1)
-    temb = jnp.repeat(temb, cols, axis=0)
-    edges = jnp.stack([latent[:, :, cols - 1], latent[:, :, 0]]).astype(F32)[:, :, :, None, :]
+    half = time_weight.shape[0] // 2
+    freqs = jnp.exp(-jnp.log(10000.0) * jnp.arange(half, dtype=F32) / half).reshape(1, half)
     vm = pl.BlockSpec(memory_space=pltpu.VMEM)
     hbm = pl.BlockSpec(memory_space=pl.ANY)
     dma = pltpu.SemaphoreType.DMA
@@ -420,14 +459,16 @@
             jax.ShapeDtypeStruct((batch, span, inner), BF16),
             jax.ShapeDtypeStruct((batch, span, inner), BF16),
         ),
-        in_specs=[vm] * 6 + [hbm] * 7,
+        in_specs=[pl.BlockSpec(memory_space=pltpu.SMEM)] + [vm] * 5 + [hbm] * 9,
         out_specs=(vm, vm, vm),
         scratch_shapes=[
             pltpu.VMEM((R, batch, rows, cols, channels), BF16),
+            pltpu.VMEM((2, batch, rows, 1, channels), F32),
             pltpu.VMEM((R, 2, batch, rows, 1, channels), F32),
+            pltpu.VMEM(time_weight.shape, BF16),
             pltpu.VMEM((3, R * rows + 2, batch * cols, channels), BF16),
             pltpu.VMEM((R * rows, batch * cols, channels), BF16),
-            pltpu.VMEM(conv_weight.shape, BF16),
+            pltpu.VMEM((3, 3, wide, channels), BF16),
             pltpu.VMEM((channels, 3 * inner), BF16),
             pltpu.VMEM((inner, channels), BF16),
             pltpu.VMEM((C, 8, channels), F32),
@@ -445,9 +486,9 @@
             pltpu.VMEM((NX, batch, span, inner), BF16),
             pltpu.VMEM((NX, batch, span, 128), F32),
             pltpu.VMEM((batch, span, inner), BF16),
-            dma((7,)),
-            dma((3, R)),
-            dma((3, R)),
+            dma((9,)),
+            dma((batch + 2, R)),
+            dma((batch + 2, R)),
             dma((3, C)),
             dma((3, C)),
             dma((2,)),
@@ -461,13 +502,15 @@
             collective_id=0, has_side_effects=True, vmem_limit_bytes=56 * 1024 * 1024
         ),
     )(
+        timestep,
+        freqs,
+        gn_gain,
+        gn_bias,
+        ln_gain,
+        conv_bias,
         latent,
-        edges,
-        temb,
-        gn_gain.reshape(1, channels),
-        gn_bias.reshape(1, channels),
-        ln_gain.reshape(1, channels),
-        conv_weight,
+        time_weight,
+        conv_weight.transpose(0, 1, 3, 2),
         q_weight,
         k_weight,
         v_weight,
@@ -475,6 +518,13 @@
         stale_keys.reshape(batch, span, inner),
         stale_values.reshape(batch, span, inner),
     )
+    mixed, fresh_k, fresh_v = pl.pallas_call(
+        finish,
+        out_shape=tuple(jax.ShapeDtypeStruct(x.shape, x.dtype) for x in (mixed, fresh_k, fresh_v)),
+        in_specs=[hbm] * 3,
+        out_specs=(hbm,) * 3,
+        scratch_shapes=[dma((3,))],
+    )(mixed, fresh_k, fresh_v)
     return (
         mixed.reshape(batch, rows, cols, channels),
         fresh_k.reshape(batch, rows, cols, inner),

time: 64.2 us -> 63.2 us (0.984)
  Pallas kernels: 45.1 us -> 61.9 us
  local copies, waits for them, and re-layouts: 16.1 us -> 0 us
  other arithmetic: 1.66 us -> 0.58 us
    pallas_call x0 -> x1, Pallas kernels: none -> 12 us  [body(): pl.pallas_call(finish, out_shape=tuple((jax.ShapeDtypeStruct(x.shape, x.d...]
    unnamed x6 -> x0, local copies, waits for them, and re-layouts: 9.77 us -> none
    pallas_call x1, Pallas kernels: 45.1 us -> 49.8 us  [body(): pl.pallas_call(functools.partial(kernel, (R, C, NX, rows, cols, channels,...]
    reshape x4 -> x0, local copies, waits for them, and re-layouts: 4.45 us -> none  [the longest x1 1.28 us: body(): gn_bias.reshape(1, channels)]
    convert_element_type x2 -> x0, other arithmetic: 1.45 us -> none  [the longest x1 0.74 us: body(): jnp.stack([latent[:, :, cols - 1], latent[:, :, 0]]).astype(F32)]
    slice x1 -> x0, local copies, waits for them, and re-layouts: 1.06 us -> none  [body(): latent[:, :, cols - 1]]
    dynamic_slice x1 -> x0, local copies, waits for them, and re-layouts: 0.76 us -> none  [body(): temb = lax.dynamic_slice_in_dim(temb, me * wide, wide, 1)]
where the time goes in v2:
time: 63.2 us; the launch traced here: 63.1 us
  Pallas kernels  61.9 us (98%)
  between operations  0.64 us (1%)
    pallas_call x1, Pallas kernels, body(): pl.pallas_call(functools.partial(kernel, (R, C, NX, rows, cols, channels,...  49.8 us
    pallas_call x1, Pallas kernels, body(): pl.pallas_call(finish, out_shape=tuple((jax.ShapeDtypeStruct(x.shape, x.d...  12 us

profile of v2, /device:TPU:0, one launch (start us, length us, event | category | flops | bytes accessed | tf_op | source)
XLA Modules:
  0.0 63.1 jit_solution(1839958362128792503)
XLA Ops:
  0.6 0.6 multiply_exponential_fusion.freq_ref
  1.2 49.8 %shard_map.157 = (bf16[2,64,640]{2,1,0:T(8,128)(2,1)}, bf16[2,64,384]{2,1,0:T(8,128)(2,1)}, bf16[2,64,384]{2,1,0:T(8,128)(2,1)}) custom-call(s32[2]{0:T(128)} %t_ref.1, f32[1,160]{1,0:T(1,128)} %multiply_exponential_fusion.freq_ref, f32[640]{0:T(1024)} %gg_ref.1, f32[640]{0:T(1024)} %gb_ref.1, f32[640]{0:T(1024)} %lg_ref.1, f32[640]{0:T(1024)} %bias_ref.1, ...), custom_call_target="tpu_custom_call" | custom-call | tf_op jit(solution)/shard_map/pallas_call | solution.py:455
  51.0 12.0 %shard_map.158 = (bf16[2,64,640]{2,1,0:T(8,128)(2,1)}, bf16[2,64,384]{2,1,0:T(8,128)(2,1)}, bf16[2,64,384]{2,1,0:T(8,128)(2,1)}) custom-call(bf16[2,64,640]{2,1,0:T(8,128)(2,1)} %get-tuple-element.9.a, bf16[2,64,384]{2,1,0:T(8,128)(2,1)} %get-tuple-element.10.b, bf16[2,64,384]{2,1,0:T(8,128)(2,1)} %get-tuple-element.11.c), custom_call_target="tpu_custom_call" | custom-call | tf_op jit(solution)/shard_map/pallas_call | solution.py:521

commit v3 on v2

--- a/solution.py
+++ b/solution.py
@@ -10,7 +10,7 @@
 HD = 64
 GROUPS = 32
 PAIR = 2
-EARLY = True
+EARLY = False
 MESH = pl.DeviceIdType.MESH
 F32 = jnp.float32
 BF16 = jnp.bfloat16
@@ -54,12 +54,10 @@
     ]
 
 
-def finish(a, b, c, x, y, z, sem):
-    copies = [pltpu.make_async_copy(s, d, sem.at[n]) for n, (s, d) in enumerate(((a, x), (b, y), (c, z)))]
-    for copy in copies:
-        copy.start()
-    for copy in copies:
-        copy.wait()
+def finish(a, b, c, x, y, z):
+    x[...] = a[...]
+    y[...] = b[...]
+    z[...] = c[...]
 
 
 def kernel(
@@ -521,9 +519,8 @@
     mixed, fresh_k, fresh_v = pl.pallas_call(
         finish,
         out_shape=tuple(jax.ShapeDtypeStruct(x.shape, x.dtype) for x in (mixed, fresh_k, fresh_v)),
-        in_specs=[hbm] * 3,
-        out_specs=(hbm,) * 3,
-        scratch_shapes=[dma((3,))],
+        in_specs=[vm] * 3,
+        out_specs=(vm,) * 3,
     )(mixed, fresh_k, fresh_v)
     return (
         mixed.reshape(batch, rows, cols, channels),

time: 63.2 us -> 47.9 us (0.76)
  the two profiles are of different devices: /device:TPU:0 before, /device:TPU:8 now
where the time goes in v3:
time: 47.9 us; the launch traced here: 47.8 us
  Pallas kernels  46.5 us (97%)
  between operations  0.64 us (1%)
  other arithmetic  0.58 us (1%)
    pallas_call x1, Pallas kernels, body(): pl.pallas_call(functools.partial(kernel, (R, C, NX, rows, cols, channels,...  44.8 us
    pallas_call x1, Pallas kernels, body(): pl.pallas_call(finish, out_shape=tuple((jax.ShapeDtypeStruct(x.shape, x.d...  1.76 us

profile of v3, /device:TPU:8, one launch (start us, length us, event | category | flops | bytes accessed | tf_op | source)
XLA Modules:
  0.0 47.8 jit_solution(6308685154793714853)
XLA Ops:
  0.6 0.6 %multiply_exponential_fusion.freq_ref = f32[1,160]{1,0:T(1,128)} fusion(), kind=kLoop, calls=%fused_computation | loop fusion | flops 160 | bytes 640 | tf_op jit(solution)/shard_map/exp | solution.py:449
  1.2 44.8 %shard_map.157 = (bf16[2,64,640]{2,1,0:T(8,128)(2,1)}, bf16[2,64,384]{2,1,0:T(8,128)(2,1)}, bf16[2,64,384]{2,1,0:T(8,128)(2,1)}) custom-call(s32[2]{0:T(128)} %t_ref.1, f32[1,160]{1,0:T(1,128)} %multiply_exponential_fusion.freq_ref, f32[640]{0:T(1024)} %gg_ref.1, f32[640]{0:T(1024)} %gb_ref.1, f32[640]{0:T(1024)} %lg_ref.1, f32[640]{0:T(1024)} %bias_ref.1, ...), custom_call_target="tpu_custom_call" | custom-call | tf_op jit(solution)/shard_map/pallas_call | solution.py:453
  46.0 1.8 %shard_map.158 = (bf16[2,64,640]{2,1,0:T(8,128)(2,1)}, bf16[2,64,384]{2,1,0:T(8,128)(2,1)}, bf16[2,64,384]{2,1,0:T(8,128)(2,1)}) custom-call(bf16[2,64,640]{2,1,0:T(8,128)(2,1)} %get-tuple-element.9.a, bf16[2,64,384]{2,1,0:T(8,128)(2,1)} %get-tuple-element.10.b, bf16[2,64,384]{2,1,0:T(8,128)(2,1)} %get-tuple-element.11.c), custom_call_target="tpu_custom_call" | custom-call | tf_op jit(solution)/shard_map/pallas_call | solution.py:519

commit v4 on v3

--- a/solution.py
+++ b/solution.py
@@ -10,7 +10,6 @@
 HD = 64
 GROUPS = 32
 PAIR = 2
-EARLY = False
 MESH = pl.DeviceIdType.MESH
 F32 = jnp.float32
 BF16 = jnp.bfloat16
@@ -40,20 +39,6 @@
     return window(ends, -1)
 
 
-def send_stale(go, kbuf, vbuf, span, C, mc, col_send, col_recv):
-    return [
-        go(
-            buf.at[:, 0:span],
-            buf.at[:, (C - d) * span : (C - d + 1) * span],
-            col_send.at[n, d],
-            col_recv.at[n, d],
-            col=lax.rem(mc + d, C),
-        )
-        for d in range(1, C)
-        for n, buf in ((1, kbuf), (2, vbuf))
-    ]
-
-
 def finish(a, b, c, x, y, z):
     x[...] = a[...]
     y[...] = b[...]
@@ -63,7 +48,6 @@
 def kernel(
     dims,
     t_ref,
-    freq_ref,
     gg_ref,
     gb_ref,
     lg_ref,
@@ -109,6 +93,8 @@
     row_recv,
     col_send,
     col_recv,
+    hop_send,
+    hop_recv,
     edge_send,
     edge_recv,
     fwd_send,
@@ -190,10 +176,40 @@
         return handed
 
     lat_out = [spread(band.at[me, b], b) for b in range(nb)]
-    if EARLY:
-        loads[5].wait()
-        loads[6].wait()
-        stale_out = send_stale(go, kbuf, vbuf, span, C, mc, col_send, col_recv)
+
+    def hops(k):
+        made = []
+        for n, buf in enumerate((kbuf, vbuf)):
+            for way, slot, dest, to, sends, takes in (
+                (0, (C - k + 1) % C, C - k, mc + 1, (mc >= k - 1) & (mc < C - 1), mc >= k),
+                (1, k - 1, k, mc + C - 1, (mc <= C - k) & (mc > 0), mc <= C - 1 - k),
+            ):
+                copy = remote(
+                    buf.at[:, slot * span : (slot + 1) * span],
+                    buf.at[:, dest * span : (dest + 1) * span],
+                    hop_send.at[k, n, way],
+                    hop_recv.at[k, n, way],
+                    col=lax.rem(to, C),
+                )
+                made.append((copy, sends, takes))
+        return made
+
+    def each(k, act, which):
+        for hop in hops(k):
+
+            @pl.when(hop[which])
+            def _(copy=hop[0]):
+                act(copy)
+
+    def send_hop(k):
+        if k < C:
+            if k > 1:
+                each(k - 1, lambda copy: copy.wait_recv(), 2)
+            each(k, lambda copy: copy.start(), 1)
+
+    loads[5].wait()
+    loads[6].wait()
+    send_hop(1)
 
     @pl.when(mc == 0)
     def _():
@@ -213,10 +229,11 @@
 
     halo_out = spread(halo.at[me], nb)
 
-    half_t = freq_ref.shape[1]
+    half_t = tw.shape[0] // 2
     line = lax.broadcasted_iota(jnp.int32, (nb * cols, half_t), 0)
     when = jnp.where(line < cols, t_ref[0], t_ref[1]).astype(F32)
-    angles = when * freq_ref[...]
+    place_t = lax.broadcasted_iota(jnp.int32, (nb * cols, half_t), 1).astype(F32)
+    angles = when * jnp.exp(-jnp.log(jnp.full((1, 1), 10000.0, F32)) * place_t / half_t)
     loads[7].wait()
     temb = jnp.dot(
         jax.nn.silu(jnp.cos(angles)).astype(BF16), tw[0:half_t, :], preferred_element_type=F32
@@ -251,10 +268,7 @@
         for d in range(1, C)
     ]
     handed = relay(halo_out[1], lambda p: halo.at[p], nb)
-    if not EARLY:
-        loads[5].wait()
-        loads[6].wait()
-        stale_out = send_stale(go, kbuf, vbuf, span, C, mc, col_send, col_recv)
+    send_hop(2)
     pick = (
         lax.broadcasted_iota(jnp.int32, (channels, wide), 0)
         == lax.broadcasted_iota(jnp.int32, (channels, wide), 1) + me * wide
@@ -297,6 +311,8 @@
             acts[t, 1 + r * rows : 1 + (r + 1) * rows] = jnp.concatenate(tap[t], axis=1).astype(BF16)
     loads[0].wait()
     for across in range(3):
+        if across:
+            send_hop(across + 2)
         for down in range(3):
             acc = acc + lax.dot_general(
                 acts[across, down : down + R * rows].reshape(R * rows * nb * cols, channels),
@@ -311,8 +327,9 @@
         to = lax.rem(me + d, R)
         h_out.append(go(hsend.at[to], hbuf.at[me], row_send.at[nb + 1, d], row_recv.at[nb + 1, d], row=to))
     hbuf[me] = hsend[me]
-    for copy in stale_out:
-        copy.wait_recv()
+    for k in range(5, C + 1):
+        send_hop(k)
+    each(C - 1, lambda copy: copy.wait_recv(), 2)
     forwards = [
         go(buf.at[:, 0 : C * span], buf.at[:, C * span : 2 * C * span], fwd_send.at[n], fwd_recv.at[n], row=mate)
         for n, buf in enumerate((kbuf, vbuf))
@@ -382,13 +399,15 @@
                 out_o[d, b, :, at] = o.astype(BF16)
 
             out_s[d, b] = attend(qin[d, b], b, 0, give)
-        to = lax.rem(me + d * PAIR, R)
-        for n, src, dst in ((1, out_o, in_o), (2, out_s, in_s)):
-            back.append(go(src.at[d], dst.at[NX - d], x_send.at[n, d], x_recv.at[n, d], row=to))
-    for copy in back:
-        copy.wait_recv()
+            to = lax.rem(me + d * PAIR, R)
+            for n, src, dst in ((1, out_o, in_o), (3, out_s, in_s)):
+                n = n + b
+                back.append((b, go(src.at[d, b], dst.at[NX - d, b], x_send.at[n, d], x_recv.at[n, d], row=to)))
     loads[4].wait()
     for b in range(nb):
+        for owner, copy in back:
+            if owner == b:
+                copy.wait_recv()
         for pair in range(inner // (2 * HD)):
             at = slice(pair * 2 * HD, (pair + 1) * 2 * HD)
 
@@ -418,6 +437,8 @@
     def _():
         to_left.wait_send()
 
+    for k in range(1, C):
+        each(k, lambda copy: copy.wait_send(), 1)
     for copy in started:
         copy.wait_send()
 
@@ -445,8 +466,6 @@
     span = rows * cols
     wide = conv_weight.shape[3]
     count_all = span * R * C * (channels // GROUPS)
-    half = time_weight.shape[0] // 2
-    freqs = jnp.exp(-jnp.log(10000.0) * jnp.arange(half, dtype=F32) / half).reshape(1, half)
     vm = pl.BlockSpec(memory_space=pltpu.VMEM)
     hbm = pl.BlockSpec(memory_space=pl.ANY)
     dma = pltpu.SemaphoreType.DMA
@@ -457,7 +476,7 @@
             jax.ShapeDtypeStruct((batch, span, inner), BF16),
             jax.ShapeDtypeStruct((batch, span, inner), BF16),
         ),
-        in_specs=[pl.BlockSpec(memory_space=pltpu.SMEM)] + [vm] * 5 + [hbm] * 9,
+        in_specs=[pl.BlockSpec(memory_space=pltpu.SMEM)] + [vm] * 4 + [hbm] * 9,
         out_specs=(vm, vm, vm),
         scratch_shapes=[
             pltpu.VMEM((R, batch, rows, cols, channels), BF16),
@@ -487,21 +506,22 @@
             dma((9,)),
             dma((batch + 2, R)),
             dma((batch + 2, R)),
-            dma((3, C)),
-            dma((3, C)),
+            dma((1, C)),
+            dma((1, C)),
+            dma((C, 2, 2)),
+            dma((C, 2, 2)),
             dma((2,)),
             dma((2,)),
             dma((2,)),
             dma((2,)),
-            dma((3, NX)),
-            dma((3, NX)),
+            dma((5, NX)),
+            dma((5, NX)),
         ],
         compiler_params=pltpu.CompilerParams(
             collective_id=0, has_side_effects=True, vmem_limit_bytes=56 * 1024 * 1024
         ),
     )(
         timestep,
-        freqs,
         gn_gain,
         gn_bias,
         ln_gain,

time: 47.9 us -> 42.5 us (0.89)
  the two profiles are of different devices: /device:TPU:8 before, /device:TPU:0 now
where the time goes in v4:
time: 42.5 us; the launch traced here: 42.3 us
  Pallas kernels  41.7 us (98%)
  between operations  0.64 us (2%)
    pallas_call x1, Pallas kernels, body(): pl.pallas_call(functools.partial(kernel, (R, C, NX, rows, cols, channels,...  39.9 us
    pallas_call x1, Pallas kernels, body(): pl.pallas_call(finish, out_shape=tuple((jax.ShapeDtypeStruct(x.shape, x.d...  1.76 us

profile of v4, /device:TPU:0, one launch (start us, length us, event | category | flops | bytes accessed | tf_op | source)
XLA Modules:
  0.0 42.3 jit_solution(11627162169919320133)
XLA Ops:
  0.6 39.9 %shard_map.157 = (bf16[2,64,640]{2,1,0:T(8,128)(2,1)}, bf16[2,64,384]{2,1,0:T(8,128)(2,1)}, bf16[2,64,384]{2,1,0:T(8,128)(2,1)}) custom-call(s32[2]{0:T(128)} %t_ref.1, f32[640]{0:T(1024)} %gg_ref.1, f32[640]{0:T(1024)} %gb_ref.1, f32[640]{0:T(1024)} %lg_ref.1, f32[640]{0:T(1024)} %bias_ref.1, bf16[2,8,8,640]{3,2,1,0:T(8,128)(2,1)} %lat_hbm.1, ...), custom_call_target="tpu_custom_call" | custom-call | tf_op jit(solution)/shard_map/pallas_call | solution.py:472
  40.6 1.8 %shard_map.158 = (bf16[2,64,640]{2,1,0:T(8,128)(2,1)}, bf16[2,64,384]{2,1,0:T(8,128)(2,1)}, bf16[2,64,384]{2,1,0:T(8,128)(2,1)}) custom-call(bf16[2,64,640]{2,1,0:T(8,128)(2,1)} %get-tuple-element.9.a, bf16[2,64,384]{2,1,0:T(8,128)(2,1)} %get-tuple-element.10.b, bf16[2,64,384]{2,1,0:T(8,128)(2,1)} %get-tuple-element.11.c), custom_call_target="tpu_custom_call" | custom-call | tf_op jit(solution)/shard_map/pallas_call | solution.py:539
